TPU v7x, 1024 devices: a whole 4x4x32 slice. The times are simulated.
1024 devices in a mesh: pipe: 8 (over y, core), expert: 32 (over z), dp: 4 (over x).
Axes of the slice: x: 4, y: 4, z: 32, core: 2. Of those that a mesh axis runs over, the one named last changes fastest.
Arguments:
- section_grad: bfloat16 [8, 16384, 7168], P('pipe', ('expert', 'dp')), may hold values from -6 to 6
- loss_grad: bfloat16 [16384, 7168], P(('expert', 'dp')), may hold values from -6 to 6
- expert_ids: int32 [8, 16384, 8], P('pipe', ('expert', 'dp')), may hold values from 0 to 255, all different within a row
- gate_values: bfloat16 [8, 16384, 8], P('pipe', ('expert', 'dp')), may hold values from 0.049804688 to 0.59765625
- down_inputs: bfloat16 [8, 4, 128, 8192], P('pipe', 'dp', None, 'expert'), may hold values from -1.59375 to 1.59375
Outputs:
- down_grad: bfloat16 [8, 7168, 8192], P('pipe', 'dp', 'expert')
Inputs may be any that keep to these rules, and one draw needn't show every extreme that they name: `expert_ids`: each row names 8 different experts; every expert is named by some row.
All inputs are finite; a program needn't handle non-finite values.
Results may differ from a plain program's by a relative error of at most 0.009.
Values may be sent and summed in bfloat16 or wider, within the bound.
No kernel may reach another device: no remote copies, remote signals or barrier semaphores. Data moves between devices by JAX's collectives and lax.ppermute only.
A program may use at most 32 MiB of HBM per device.

v0:
```python
import jax
import jax.numpy as jnp
from jax import lax
from jax.sharding import PartitionSpec as P

ROUTED = 256
TOPK = 8
SPLIT = 4


def from_behind(value, axis, steps):
    count = lax.axis_size(axis)
    leading, last = (max(0, -steps), min(count, count - steps))
    return lax.ppermute(value, axis, [(source, source + steps) for source in range(leading, last)])


def compact_rows(id_block, gate_block, grad_rows, experts, capacity):
    flat_ids = id_block.reshape(-1)
    onehot = (flat_ids[:, None] == jnp.arange(experts, dtype=jnp.int32)[None, :]).astype(jnp.int32)
    before = jnp.cumsum(onehot, axis=0) - onehot
    ranks = jnp.sum(before * onehot, axis=1)
    retained = (flat_ids < experts) & (ranks < capacity)
    target = jnp.where(retained, flat_ids * capacity + ranks, -1).reshape(id_block.shape)
    wanted = jnp.arange(experts * capacity, dtype=jnp.int32)
    matches = target[None, :, :] == wanted[:, None, None]
    selector = jnp.sum(
        jnp.where(matches, gate_block[None, :, :].astype(jnp.float32), 0.0), axis=2
    ).astype(jnp.bfloat16)
    return jnp.dot(selector, grad_rows, preferred_element_type=jnp.float32).astype(jnp.bfloat16)


def local(section_grad, loss_grad, expert_ids, gate_values, down_inputs):
    expert_count = lax.axis_size("expert")
    experts = expert_count // SPLIT
    tokens_dev = section_grad.shape[1]
    model_width = section_grad.shape[2]
    capacity = tokens_dev * TOPK // ROUTED
    last_section = lax.axis_index("pipe") == lax.axis_size("pipe") - 1
    received = from_behind(section_grad[0], "pipe", -1)
    upstream = jnp.where(last_section, loss_grad, received)
    compact = compact_rows(expert_ids[0], gate_values[0], upstream, experts, capacity)
    spread_rows = jnp.broadcast_to(
        compact.reshape(experts, 1, capacity, model_width), (experts, SPLIT, capacity, model_width)
    )
    outgoing = spread_rows.reshape(expert_count, capacity, model_width)
    arrived = lax.all_to_all(outgoing, "expert", split_axis=0, concat_axis=0, tiled=True)
    slot_rows = arrived.reshape(expert_count * capacity, model_width)
    saved_inputs = down_inputs[0, 0]
    summed = lax.psum_scatter(
        lax.dot_general(
            slot_rows, saved_inputs, (((0,), (0,)), ((), ())), preferred_element_type=jnp.float32
        ).astype(jnp.bfloat16),
        "dp",
        scatter_dimension=0,
        tiled=True,
    )
    return summed[None]


def solution(mesh):
    in_specs = (
        P("pipe", ("expert", "dp"), None),
        P(("expert", "dp"), None),
        P("pipe", ("expert", "dp"), None),
        P("pipe", ("expert", "dp"), None),
        P("pipe", "dp", None, "expert"),
    )
    out_specs = P("pipe", "dp", "expert")
    return jax.shard_map(local, mesh=mesh, in_specs=in_specs, out_specs=out_specs, check_vma=False)
```

profile of v0, /device:TPU:1, one launch (start us, length us, event | category | flops | bytes accessed | tf_op | source)
XLA Modules:
  0.0 293.6 jit_solution(17038227905716800036)
XLA Ops:
  6.5 0.0 copy-start
  6.5 0.0 reduce-scatter.2.cloned.1.call-start
  6.5 16.1 %collective-permute-start = (bf16[128,7168]{1,0:T(8,128)(2,1)}, bf16[128,7168]{1,0:T(8,128)(2,1)S(1)}, u32[]{:S(2)}, u32[]{:S(2)}) collective-permute-start(bf16[128,7168]{1,0:T(8,128)(2,1)} %bitcast.34), channel_id=1, source_target_pairs={{128,0},{256,128},{384,256},{512,384},{640,512},{768,640},{896,768... | collective-permute-start | bytes 5505032 | tf_op jit(solution)/shard_map/ppermute | solution.py:14
  22.7 0.8 copy.22
  23.5 0.1 eq.47
  23.6 0.1 eq.43
  23.7 2.3 reduce-window.6
  26.0 0.3 slice_reduce_fusion
  26.2 0.2 reduce-window.9
  26.4 0.1 add_bitcast_fusion
  26.5 0.1 reduce_sum.21
  26.6 0.7 bitcast_convert_fusion
  27.4 0.7 select_bitcast_fusion
  28.0 0.1 select_reduce_fusion
  28.1 4.3 %collective-permute-done = bf16[128,7168]{1,0:T(8,128)(2,1)S(1)} collective-permute-done((bf16[128,7168]{1,0:T(8,128)(2,1)}, bf16[128,7168]{1,0:T(8,128)(2,1)S(1)}, u32[]{:S(2)}, u32[]{:S(2)}) %collective-permute-start) | collective-permute-done | bytes 1835040 | tf_op jit(solution)/shard_map/ppermute | solution.py:14
  32.4 0.5 convolution_convert_fusion.1
  32.8 0.2 broadcast_in_dim.38
  33.0 0.5 broadcast_in_dim.39
  33.6 188.9 %all_to_all.5 = bf16[32,4,7168]{2,1,0:T(4,128)(2,1)} all-to-all(bf16[32,4,7168]{2,1,0:T(4,128)(2,1)S(1)} %bitcast.32), channel_id=1, replica_groups=mesh['pipe'=8,'expert'=32,'dp'=4] {'expert'}, dimensions={0} | all-to-all | bytes 3670016 | tf_op jit(solution)/shard_map/all_to_all | solution.py:46
  222.5 2.9 %reshape.37 = bf16[128,7168]{1,0:T(8,128)(2,1)S(1)} reshape(bf16[32,4,7168]{2,1,0:T(4,128)(2,1)} %all_to_all.5) | data formatting | bytes 3670016 | tf_op jit(solution)/shard_map/reshape | solution.py:47
  225.4 0.0 copy-done
  225.4 2.9 %convolution_convert_fusion = bf16[7168,256]{1,0:T(8,128)(2,1)} fusion(bf16[128,7168]{1,0:T(8,128)(2,1)S(1)} %reshape.37, bf16[1,1,128,256]{3,2,1,0:T(8,128)(2,1)S(1)} %copy-done), kind=kOutput, calls=%fused_computation | convolution fusion | flops 471597056 | bytes 5570560 | tf_op jit(solution)/shard_map/dot_general | solution.py:50
  228.4 0.0 reduce-scatter.2.cloned.1.call-update
  228.4 58.3 %reduce-scatter.2.cloned.1.call-done = bf16[1792,256]{1,0:T(8,128)(2,1)} async-done(((bf16[7168,256]{1,0:T(8,128)(2,1)}), bf16[1792,256]{1,0:T(8,128)(2,1)}) %reduce-scatter.2.cloned.1.call-update) | async-done | bytes 917520 | tf_op jit(solution)/shard_map/reduce_scatter | solution.py:49
  (3 shorter events, 0.1 us)
Async XLA Ops:
  6.5 218.9 %copy-start = (bf16[1,1,128,256]{3,2,1,0:T(8,128)(2,1)S(1)}, bf16[1,1,128,256]{3,2,1,0:T(8,128)(2,1)}, u32[]{:S(2)}) copy-start(bf16[1,1,128,256]{3,2,1,0:T(8,128)(2,1)} %param.9) | copy-start | bytes 196612
  6.5 280.2 %reduce-scatter.2.cloned.1.call-start = ((), (), s32[]{:S(2)}) async-start(), calls=%async_computation.2 | async-start | bytes 4587520 | tf_op jit(solution)/shard_map/reduce_scatter | solution.py:49
  6.5 25.8 %collective-permute-start = (bf16[128,7168]{1,0:T(8,128)(2,1)}, bf16[128,7168]{1,0:T(8,128)(2,1)S(1)}, u32[]{:S(2)}, u32[]{:S(2)}) collective-permute-start(bf16[128,7168]{1,0:T(8,128)(2,1)} %bitcast.34), channel_id=1, source_target_pairs={{128,0},{256,128},{384,256},{512,384},{640,512},{768,640},{896,768... | collective-permute-start | bytes 5505032 | tf_op jit(solution)/shard_map/ppermute | solution.py:14
Sparse Core Ops, SparseCore 0:
  228.5 58.1 reduce-scatter.1
where the time goes:
time: 294 us
  blocking collectives  189 us (64%)
  waiting for transfers between devices  62.6 us (21%)
  starting transfers between devices  16.1 us (5%)
  between operations  13.5 us (5%)
  local copies, waits for them, and re-layouts  5.03 us (2%)
  other arithmetic  3.99 us (1%)
  matrix products  3.43 us (1%)
    all_to_all x1, blocking collectives, local(): lax.all_to_all(outgoing, 'expert', split_axis=0, concat_axis=0, tiled=True)  189 us
    reduce_scatter x1, waiting for transfers between devices, local(): lax.psum_scatter(lax.dot_general(slot_rows, saved_inputs, (((0,), (0,)),...  58.3 us
    ppermute x1, starting transfers between devices, from_behind(): lax.ppermute(value, axis, [(source, source + steps) for source in range(l...  16.1 us
  transfers between devices with their start and end apart: 2, of which 2 were waited for; matrix products, arithmetic and copies ran while one was open for 2% of the time, Pallas kernels for 0%

commit v1 on v0

v1 whole, which is shorter than its diff:
```python
import jax
import jax.numpy as jnp
from jax import lax
from jax.experimental import pallas as pl
from jax.experimental.pallas import tpu as pltpu
from jax.sharding import PartitionSpec as P

ROUTED = 256
TOPK = 8
SPLIT = 4
LANES = 128
HALF = 64
VMEM = pltpu.MemorySpace.VMEM
SMEM = pltpu.MemorySpace.SMEM


def select_kernel(ids_ref, gates_ref, out_ref):
    rows, tokens = out_ref.shape
    experts = rows // 4
    ids = ids_ref[0]
    gates = gates_ref[0].astype(jnp.float32)
    row = lax.broadcasted_iota(jnp.int32, (tokens, tokens), 1)
    expert = jnp.where(row < rows, (row >> 1) % experts, -1)
    slot = 2 * (row // (2 * experts)) + (row & 1)
    hit = jnp.zeros((tokens, tokens), jnp.float32)
    gate = jnp.zeros((tokens, tokens), jnp.float32)
    for k in range(ids.shape[1]):
        match = ids[:, k : k + 1] == expert
        hit = jnp.where(match, 1.0, hit)
        gate = jnp.where(match, gates[:, k : k + 1], gate)
    token = lax.broadcasted_iota(jnp.int32, (tokens, tokens), 0)
    earlier = jnp.where(row < token, 1.0, 0.0).astype(jnp.bfloat16)
    rank = jnp.dot(earlier, hit.astype(jnp.bfloat16), preferred_element_type=jnp.float32)
    chosen = jnp.where((hit > 0.0) & (rank == slot.astype(jnp.float32)), gate, 0.0)
    out_ref[...] = chosen.T[:rows].astype(jnp.bfloat16)


def compact_kernel(selector_ref, rows_ref, out_ref):
    quarters, subs, lines, width = out_ref.shape
    lane = lax.broadcasted_iota(jnp.int32, (lines, LANES), 1)
    low = lane < HALF
    selector = selector_ref[...]
    for d in range(quarters):
        for u in range(subs // 2):
            begin = (d * (subs // 2) + u) * width
            found = jnp.dot(selector, rows_ref[:, begin : begin + width], preferred_element_type=jnp.float32)
            for t in range(width // LANES):
                first = found[:lines, t * LANES : (t + 1) * LANES]
                second = found[lines:, t * LANES : (t + 1) * LANES]
                left = jnp.where(low, first, pltpu.roll(second, HALF, 1))
                right = jnp.where(low, pltpu.roll(first, HALF, 1), second)
                out_ref[d, 2 * u, :, t * LANES : (t + 1) * LANES] = left.astype(jnp.bfloat16)
                out_ref[d, 2 * u + 1, :, t * LANES : (t + 1) * LANES] = right.astype(jnp.bfloat16)


def product_kernel(place_ref, slots_ref, near_ref, far_ref, *out_refs):
    groups, lines, width = slots_ref.shape
    own = place_ref[0]
    slots = jnp.concatenate([slots_ref[own ^ j] for j in range(groups)], axis=0)
    turned = slots.astype(jnp.float32).T.astype(jnp.bfloat16)
    tiles = width // LANES
    parts = [
        jnp.concatenate([turned[t * LANES + h * HALF : t * LANES + (h + 1) * HALF] for t in range(tiles)], axis=0)
        for h in range(2)
    ]
    for i, out_ref in enumerate(out_refs):
        total = None
        for h in range(2):
            weights = jnp.concatenate(
                [near_ref[0, i, h], near_ref[1, i, h], far_ref[0, i, h], far_ref[1, i, h]], axis=0
            )
            term = jnp.dot(parts[h], weights, preferred_element_type=jnp.float32)
            total = term if total is None else total + term
        out_ref[...] = total.astype(jnp.bfloat16).reshape(out_ref.shape)


def place_kernel(place_ref, *refs):
    out_ref = refs[-1]
    own = place_ref[0]
    for i, block_ref in enumerate(refs[:-1]):
        member = own ^ i
        out_ref[member >> 1, :, member & 1] = block_ref[...]


def call(kernel, out_shapes, operands, scalars=0):
    specs = [pl.BlockSpec(memory_space=SMEM if n < scalars else VMEM) for n in range(len(operands))]
    single = not isinstance(out_shapes, list)
    shapes = [out_shapes] if single else out_shapes
    out = pl.pallas_call(
        kernel,
        in_specs=specs,
        out_specs=[pl.BlockSpec(memory_space=VMEM) for _ in shapes],
        out_shape=[jax.ShapeDtypeStruct(shape, jnp.bfloat16) for shape in shapes],
        name=kernel.__name__,
    )(*operands)
    return out[0] if single else out


def shift(value, axis, steps):
    count = lax.axis_size(axis)
    return lax.ppermute(value, axis, [(n, (n + steps) % count) for n in range(count)])


def swap(value, axis, mask):
    return lax.ppermute(value, axis, [(n, n ^ mask) for n in range(lax.axis_size(axis))])


def local(section_grad, loss_grad, expert_ids, gate_values, down_inputs):
    expert_count = lax.axis_size("expert")
    groups = lax.axis_size("dp")
    experts = expert_count // SPLIT
    tokens = section_grad.shape[1]
    model_width = section_grad.shape[2]
    columns = down_inputs.shape[3]
    capacity = tokens * TOPK // ROUTED
    width = model_width // (2 * groups)
    tiles = width // LANES

    selector = call(select_kernel, (experts * capacity, tokens), (expert_ids, gate_values))
    selector = shift(selector, "pipe", 1)
    first = lax.axis_index("pipe") == 0
    upstream = jnp.where(first, loss_grad, section_grad[0])
    picked = call(compact_kernel, (groups, SPLIT, experts * 2, width), (selector, upstream))
    picked = shift(picked, "pipe", -1)
    outgoing = picked.reshape(groups, SPLIT, experts, 2, width).transpose(0, 2, 1, 3, 4)
    outgoing = outgoing.reshape(groups * expert_count, 2, width)
    arrived = lax.all_to_all(outgoing, ("dp", "expert"), split_axis=0, concat_axis=0, tiled=True)
    slots = arrived.reshape(groups, expert_count * 2, width)

    saved = down_inputs[0, 0].reshape(expert_count, 2, 2, columns).transpose(1, 0, 2, 3)
    saved = saved.reshape(1, 2, expert_count * 2, columns)
    saved = jnp.concatenate([saved, swap(saved, "expert", 1)], axis=0)
    saved = jnp.concatenate([saved, swap(saved, "expert", 2)], axis=0)[None]
    near = jnp.concatenate([saved, swap(saved, "dp", 1)], axis=0)
    far = swap(near, "dp", 2)

    block = (tiles, HALF, columns)
    terms = call(
        product_kernel, [block] * SPLIT, (lax.axis_index("dp").reshape(1), slots, near, far), scalars=1
    )
    blocks = [terms[0]] + [swap(terms[i], "expert", i) for i in range(1, SPLIT)]
    member = (lax.axis_index("expert") % SPLIT).reshape(1)
    out = call(place_kernel, (2, tiles, 2, HALF, columns), (member, *blocks), scalars=1)
    return out.reshape(1, 2 * width, columns)


def solution(mesh):
    in_specs = (
        P("pipe", ("expert", "dp"), None),
        P(("expert", "dp"), None),
        P("pipe", ("expert", "dp"), None),
        P("pipe", ("expert", "dp"), None),
        P("pipe", "dp", None, "expert"),
    )
    out_specs = P("pipe", "dp", "expert")
    return jax.shard_map(local, mesh=mesh, in_specs=in_specs, out_specs=out_specs, check_vma=False)
```

time: 294 us -> 165 us (0.56)
  the two profiles are of different devices: /device:TPU:1 before, /device:TPU:46 now
where the time goes in v1:
time: 165 us; the launch traced here: 164 us
  waiting for transfers between devices  83.8 us (51%)
  starting transfers between devices  60.1 us (36%)
  Pallas kernels  9.75 us (6%)
  local copies, waits for them, and re-layouts  7.23 us (4%)
  other arithmetic  3.04 us (2%)
    ppermute x7, waiting for transfers between devices, swap(): lax.ppermute(value, axis, [(n, n ^ mask) for n in range(lax.axis_size(axi...  77.1 us
    all_to_all x1, starting transfers between devices, local(): lax.all_to_all(outgoing, ('dp', 'expert'), split_axis=0, concat_axis=0, t...  32.7 us
    ppermute x7, starting transfers between devices, swap(): lax.ppermute(value, axis, [(n, n ^ mask) for n in range(lax.axis_size(axi...  26 us
    pallas_call x4, Pallas kernels, call(): pl.pallas_call(kernel, in_specs=specs, out_specs=[pl.BlockSpec(memory_spa...  9.75 us
    ppermute x2, waiting for transfers between devices, shift(): lax.ppermute(value, axis, [(n, (n + steps) % count) for n in range(count)])  6.65 us
    unnamed x16, local copies, waits for them, and re-layouts  4.9 us
  transfers between devices with their start and end apart: 10, of which 9 were waited for; matrix products, arithmetic and copies ran while one was open for 3% of the time, Pallas kernels for 0%

profile of v1, /device:TPU:46, one launch (start us, length us, event | category | flops | bytes accessed | tf_op | source)
XLA Modules:
  0.0 164.0 jit_solution(9835398563492112190)
XLA Ops:
  0.0 1.4 copy.6.ids_ref
  1.4 1.4 copy.7.gates_ref
  2.8 1.9 %select_kernel.1 = bf16[32,128]{1,0:T(8,128)(2,1)} custom-call(s32[1,128,8]{2,1,0:T(8,128)} %copy.6.ids_ref, bf16[1,128,8]{2,1,0:T(8,128)(2,1)} %copy.7.gates_ref), custom_call_target="tpu_custom_call" | custom-call | tf_op jit(solution)/shard_map/select_kernel/pallas_call | solution.py:89
  4.7 3.0 %bitcast_select_fusion.rows_ref = bf16[128,7168]{1,0:T(8,128)(2,1)} fusion(bf16[128,7168]{1,0:T(8,128)(2,1)} %param.6, bf16[1,128,7168]{2,1,0:T(8,128)(2,1)} %param.5, pred[]{:T(512)S(6)} %eq.5), kind=kLoop, calls=%fused_computation | loop fusion | flops 917504 | bytes 5505025 | tf_op jit(solution)/shard_map/jit(_where)/select_n | solution.py:122
  8.6 2.8 %compact_kernel.1 = bf16[4,4,16,896]{3,2,1,0:T(8,128)(2,1)} custom-call(bf16[32,128]{1,0:T(8,128)(2,1)} %copy-done.6, bf16[128,7168]{1,0:T(8,128)(2,1)} %bitcast_select_fusion.rows_ref), custom_call_target="tpu_custom_call" | custom-call | tf_op jit(solution)/shard_map/compact_kernel/pallas_call | solution.py:89
  11.4 1.4 collective-permute-start.1
  12.8 6.3 %collective-permute-done.1 = bf16[4,4,16,896]{3,2,1,0:T(8,128)(2,1)S(1)} collective-permute-done((bf16[4,4,16,896]{3,2,1,0:T(8,128)(2,1)}, bf16[4,4,16,896]{3,2,1,0:T(8,128)(2,1)S(1)}, u32[]{:S(2)}, u32[]{:S(2)}) %collective-permute-start.1) | collective-permute-done | bytes 458784 | tf_op jit(solution)/shard_map/ppermute | solution.py:101
  19.3 1.1 copy.8
  20.4 32.7 %all-to-all-start = ((bf16[128,2,896]{2,1,0:T(2,128)(2,1)}), bf16[128,2,896]{2,1,0:T(2,128)(2,1)S(1)}, u32[]{:S(2)}, u32[]{:S(2)}) async-start(bf16[128,2,896]{2,1,0:T(2,128)(2,1)} %bitcast.4), calls=%async_computation | async-start | bytes 917504 | tf_op jit(solution)/shard_map/all_to_all | solution.py:127
  53.2 2.5 %collective-permute-start.2 = (bf16[1,2,64,256]{3,2,1,0:T(8,128)(2,1)S(1)}, bf16[1,2,64,256]{3,2,1,0:T(8,128)(2,1)S(1)}, u32[]{:S(2)}, u32[]{:S(2)}) collective-permute-start(bf16[1,2,64,256]{3,2,1,0:T(8,128)(2,1)S(1)} %reshape.26), channel_id=1, source_target_pairs={{0,4},{4,0},{8,12},{12,8},{16,20},{20,16},{24,28},{28,24},{32,36},... | collective-permute-start | bytes 196616 | tf_op jit(solution)/shard_map/ppermute | solution.py:105
  55.7 34.3 %collective-permute-done.2 = bf16[1,2,64,256]{3,2,1,0:T(8,128)(2,1)S(1)} collective-permute-done((bf16[1,2,64,256]{3,2,1,0:T(8,128)(2,1)S(1)}, bf16[1,2,64,256]{3,2,1,0:T(8,128)(2,1)S(1)}, u32[]{:S(2)}, u32[]{:S(2)}) %collective-permute-start.2) | collective-permute-done | bytes 65568 | tf_op jit(solution)/shard_map/ppermute | solution.py:105
  90.0 7.9 %collective-permute-start.3 = (bf16[2,2,64,256]{3,2,1,0:T(8,128)(2,1)S(1)}, bf16[2,2,64,256]{3,2,1,0:T(8,128)(2,1)S(1)}, u32[]{:S(2)}, u32[]{:S(2)}) collective-permute-start(bf16[2,2,64,256]{3,2,1,0:T(8,128)(2,1)S(1)} %pad_maximum_fusion.1), channel_id=1, source_target_pairs={{0,8},{4,12},{8,0},{12,4},{16,24},{20,28},{24,16},{28,20},{32,40},... | collective-permute-start | bytes 393224 | tf_op jit(solution)/shard_map/ppermute | solution.py:105
  97.9 5.6 %collective-permute-done.3 = bf16[2,2,64,256]{3,2,1,0:T(8,128)(2,1)S(1)} collective-permute-done((bf16[2,2,64,256]{3,2,1,0:T(8,128)(2,1)S(1)}, bf16[2,2,64,256]{3,2,1,0:T(8,128)(2,1)S(1)}, u32[]{:S(2)}, u32[]{:S(2)}) %collective-permute-start.3) | collective-permute-done | bytes 131104 | tf_op jit(solution)/shard_map/ppermute | solution.py:105
  103.5 2.5 %collective-permute-start.4 = (bf16[1,4,2,64,256]{4,3,2,1,0:T(8,128)(2,1)S(1)}, bf16[1,4,2,64,256]{4,3,2,1,0:T(8,128)(2,1)S(1)}, u32[]{:S(2)}, u32[]{:S(2)}) collective-permute-start(bf16[1,4,2,64,256]{4,3,2,1,0:T(8,128)(2,1)S(1)} %maximum_bitcast_fusion), channel_id=1, source_target_pairs={{0,1},{1,0},{2,3},{3,2},{4,5},{5,4},{6,7},{7,6},{8,9},{9,8},{10,11... | collective-permute-start | bytes 786440 | tf_op jit(solution)/shard_map/ppermute | solution.py:105
  106.0 7.7 %collective-permute-done.4 = bf16[1,4,2,64,256]{4,3,2,1,0:T(8,128)(2,1)S(1)} collective-permute-done((bf16[1,4,2,64,256]{4,3,2,1,0:T(8,128)(2,1)S(1)}, bf16[1,4,2,64,256]{4,3,2,1,0:T(8,128)(2,1)S(1)}, u32[]{:S(2)}, u32[]{:S(2)}) %collective-permute-start.4) | collective-permute-done | bytes 262176 | tf_op jit(solution)/shard_map/ppermute | solution.py:105
  113.8 2.9 %collective-permute-start.5 = (bf16[2,4,2,64,256]{4,3,2,1,0:T(8,128)(2,1)S(1)}, bf16[2,4,2,64,256]{4,3,2,1,0:T(8,128)(2,1)S(1)}, u32[]{:S(2)}, u32[]{:S(2)}) collective-permute-start(bf16[2,4,2,64,256]{4,3,2,1,0:T(8,128)(2,1)S(1)} %pad_maximum_fusion.near_ref), channel_id=1, source_target_pairs={{0,2},{1,3},{2,0},{3,1},{4,6},{5,7},{6,4},{7,5},{8,10},{9,11},{10,... | collective-permute-start | bytes 1572872 | tf_op jit(solution)/shard_map/ppermute | solution.py:105
  117.7 12.5 %collective-permute-done.5.far_ref = bf16[2,4,2,64,256]{4,3,2,1,0:T(8,128)(2,1)S(1)} collective-permute-done((bf16[2,4,2,64,256]{4,3,2,1,0:T(8,128)(2,1)S(1)}, bf16[2,4,2,64,256]{4,3,2,1,0:T(8,128)(2,1)S(1)}, u32[]{:S(2)}, u32[]{:S(2)}) %collective-permute-start.5) | collective-permute-done | bytes 524320 | tf_op jit(solution)/shard_map/ppermute | solution.py:105
  131.0 2.8 %product_kernel.1 = (bf16[7,64,256]{2,1,0:T(8,128)(2,1)}, bf16[7,64,256]{2,1,0:T(8,128)(2,1)}, bf16[7,64,256]{2,1,0:T(8,128)(2,1)}, bf16[7,64,256]{2,1,0:T(8,128)(2,1)}) custom-call(s32[1]{0:T(128)} %bitcast.1.place_ref, bf16[4,64,896]{2,1,0:T(8,128)(2,1)} %reshape.25.slots_ref, bf16[2,4,2,64,256]{4,3,2,1,0:T(8,128)(2,1)} %copy-done, ...), custom_call_target="tpu_custom_call" | custom-call | tf_op jit(solution)/shard_map/product_kernel/pallas_call | solution.py:89
  133.8 4.9 %collective-permute-start.6 = (bf16[7,64,256]{2,1,0:T(8,128)(2,1)}, bf16[7,64,256]{2,1,0:T(8,128)(2,1)S(1)}, u32[]{:S(2)}, u32[]{:S(2)}) collective-permute-start(bf16[7,64,256]{2,1,0:T(8,128)(2,1)} %get-tuple-element.10), channel_id=1, source_target_pairs={{0,4},{4,0},{8,12},{12,8},{16,20},{20,16},{24,28},{28,24},{32,36},... | collective-permute-start | bytes 688136 | tf_op jit(solution)/shard_map/ppermute | solution.py:105
  138.7 2.3 %collective-permute-start.7 = (bf16[7,64,256]{2,1,0:T(8,128)(2,1)}, bf16[7,64,256]{2,1,0:T(8,128)(2,1)S(1)}, u32[]{:S(2)}, u32[]{:S(2)}) collective-permute-start(bf16[7,64,256]{2,1,0:T(8,128)(2,1)} %get-tuple-element.11), channel_id=1, source_target_pairs={{0,8},{4,12},{8,0},{12,4},{16,24},{20,28},{24,16},{28,20},{32,40},... | collective-permute-start | bytes 688136 | tf_op jit(solution)/shard_map/ppermute | solution.py:105
  141.0 3.0 %collective-permute-start.8 = (bf16[7,64,256]{2,1,0:T(8,128)(2,1)}, bf16[7,64,256]{2,1,0:T(8,128)(2,1)S(1)}, u32[]{:S(2)}, u32[]{:S(2)}) collective-permute-start(bf16[7,64,256]{2,1,0:T(8,128)(2,1)} %get-tuple-element.12), channel_id=1, source_target_pairs={{0,12},{4,8},{8,4},{12,0},{16,28},{20,24},{24,20},{28,16},{32,44},... | collective-permute-start | bytes 688136 | tf_op jit(solution)/shard_map/ppermute | solution.py:105
  144.6 11.8 %collective-permute-done.7.refs_2_ = bf16[7,64,256]{2,1,0:T(8,128)(2,1)S(1)} collective-permute-done((bf16[7,64,256]{2,1,0:T(8,128)(2,1)}, bf16[7,64,256]{2,1,0:T(8,128)(2,1)S(1)}, u32[]{:S(2)}, u32[]{:S(2)}) %collective-permute-start.7) | collective-permute-done | bytes 229408 | tf_op jit(solution)/shard_map/ppermute | solution.py:105
  156.4 4.7 %collective-permute-done.8.refs_3_ = bf16[7,64,256]{2,1,0:T(8,128)(2,1)S(1)} collective-permute-done((bf16[7,64,256]{2,1,0:T(8,128)(2,1)}, bf16[7,64,256]{2,1,0:T(8,128)(2,1)S(1)}, u32[]{:S(2)}, u32[]{:S(2)}) %collective-permute-start.8) | collective-permute-done | bytes 229408 | tf_op jit(solution)/shard_map/ppermute | solution.py:105
  161.8 2.3 %place_kernel.1 = bf16[2,7,2,64,256]{4,3,2,1,0:T(8,128)(2,1)} custom-call(s32[1]{0:T(128)} %bitcast.place_ref, bf16[7,64,256]{2,1,0:T(8,128)(2,1)} %get-tuple-element.9.refs_0_, bf16[7,64,256]{2,1,0:T(8,128)(2,1)} %copy-done.2, bf16[7,64,256]{2,1,0:T(8,128)(2,1)} %copy-done.3, bf16[7,64,256]{2,1,0:T(8,128)(2,1)} %copy-done.4), custom_call_target="tpu_custom_call" | custom-call | tf_op jit(solution)/shard_map/place_kernel/pallas_call | solution.py:89
  (26 shorter events, 4.4 us)
Async XLA Ops:
  4.7 3.3 %collective-permute-start = (bf16[32,128]{1,0:T(8,128)(2,1)}, bf16[32,128]{1,0:T(8,128)(2,1)S(1)}, u32[]{:S(2)}, u32[]{:S(2)}) collective-permute-start(bf16[32,128]{1,0:T(8,128)(2,1)} %select_kernel.1), channel_id=1, source_target_pairs={{0,128},{128,256},{256,384},{384,512},{512,640},{640,768},{768,896... | collective-permute-start | bytes 24584 | tf_op jit(solution)/shard_map/ppermute | solution.py:101
  8.0 0.6 copy-start.6
  11.4 41.7 %copy-start.5 = (bf16[1,1,128,256]{3,2,1,0:T(8,128)(2,1)S(1)}, bf16[1,1,128,256]{3,2,1,0:T(8,128)(2,1)}, u32[]{:S(2)}) copy-start(bf16[1,1,128,256]{3,2,1,0:T(8,128)(2,1)} %param.9) | copy-start | bytes 196612
  11.4 7.7 %collective-permute-start.1 = (bf16[4,4,16,896]{3,2,1,0:T(8,128)(2,1)}, bf16[4,4,16,896]{3,2,1,0:T(8,128)(2,1)S(1)}, u32[]{:S(2)}, u32[]{:S(2)}) collective-permute-start(bf16[4,4,16,896]{3,2,1,0:T(8,128)(2,1)} %compact_kernel.1), channel_id=1, source_target_pairs={{0,896},{128,0},{256,128},{384,256},{512,384},{640,512},{768,640},... | collective-permute-start | bytes 1376264 | tf_op jit(solution)/shard_map/ppermute | solution.py:101
  20.4 96.4 %all-to-all-start = ((bf16[128,2,896]{2,1,0:T(2,128)(2,1)}), bf16[128,2,896]{2,1,0:T(2,128)(2,1)S(1)}, u32[]{:S(2)}, u32[]{:S(2)}) async-start(bf16[128,2,896]{2,1,0:T(2,128)(2,1)} %bitcast.4), calls=%async_computation | async-start | bytes 917504 | tf_op jit(solution)/shard_map/all_to_all | solution.py:127
  53.2 36.8 %collective-permute-start.2 = (bf16[1,2,64,256]{3,2,1,0:T(8,128)(2,1)S(1)}, bf16[1,2,64,256]{3,2,1,0:T(8,128)(2,1)S(1)}, u32[]{:S(2)}, u32[]{:S(2)}) collective-permute-start(bf16[1,2,64,256]{3,2,1,0:T(8,128)(2,1)S(1)} %reshape.26), channel_id=1, source_target_pairs={{0,4},{4,0},{8,12},{12,8},{16,20},{20,16},{24,28},{28,24},{32,36},... | collective-permute-start | bytes 196616 | tf_op jit(solution)/shard_map/ppermute | solution.py:105
  90.0 13.4 %collective-permute-start.3 = (bf16[2,2,64,256]{3,2,1,0:T(8,128)(2,1)S(1)}, bf16[2,2,64,256]{3,2,1,0:T(8,128)(2,1)S(1)}, u32[]{:S(2)}, u32[]{:S(2)}) collective-permute-start(bf16[2,2,64,256]{3,2,1,0:T(8,128)(2,1)S(1)} %pad_maximum_fusion.1), channel_id=1, source_target_pairs={{0,8},{4,12},{8,0},{12,4},{16,24},{20,28},{24,16},{28,20},{32,40},... | collective-permute-start | bytes 393224 | tf_op jit(solution)/shard_map/ppermute | solution.py:105
  103.5 10.2 %collective-permute-start.4 = (bf16[1,4,2,64,256]{4,3,2,1,0:T(8,128)(2,1)S(1)}, bf16[1,4,2,64,256]{4,3,2,1,0:T(8,128)(2,1)S(1)}, u32[]{:S(2)}, u32[]{:S(2)}) collective-permute-start(bf16[1,4,2,64,256]{4,3,2,1,0:T(8,128)(2,1)S(1)} %maximum_bitcast_fusion), channel_id=1, source_target_pairs={{0,1},{1,0},{2,3},{3,2},{4,5},{5,4},{6,7},{7,6},{8,9},{9,8},{10,11... | collective-permute-start | bytes 786440 | tf_op jit(solution)/shard_map/ppermute | solution.py:105
  113.7 16.4 %copy-start = (bf16[2,4,2,64,256]{4,3,2,1,0:T(8,128)(2,1)}, bf16[2,4,2,64,256]{4,3,2,1,0:T(8,128)(2,1)S(1)}, u32[]{:S(2)}) copy-start(bf16[2,4,2,64,256]{4,3,2,1,0:T(8,128)(2,1)S(1)} %pad_maximum_fusion.near_ref) | copy-start | bytes 1572868
  113.8 16.4 %collective-permute-start.5 = (bf16[2,4,2,64,256]{4,3,2,1,0:T(8,128)(2,1)S(1)}, bf16[2,4,2,64,256]{4,3,2,1,0:T(8,128)(2,1)S(1)}, u32[]{:S(2)}, u32[]{:S(2)}) collective-permute-start(bf16[2,4,2,64,256]{4,3,2,1,0:T(8,128)(2,1)S(1)} %pad_maximum_fusion.near_ref), channel_id=1, source_target_pairs={{0,2},{1,3},{2,0},{3,1},{4,6},{5,7},{6,4},{7,5},{8,10},{9,11},{10,... | collective-permute-start | bytes 1572872 | tf_op jit(solution)/shard_map/ppermute | solution.py:105
  130.2 0.8 copy-start.1
  133.8 10.8 %collective-permute-start.6 = (bf16[7,64,256]{2,1,0:T(8,128)(2,1)}, bf16[7,64,256]{2,1,0:T(8,128)(2,1)S(1)}, u32[]{:S(2)}, u32[]{:S(2)}) collective-permute-start(bf16[7,64,256]{2,1,0:T(8,128)(2,1)} %get-tuple-element.10), channel_id=1, source_target_pairs={{0,4},{4,0},{8,12},{12,8},{16,20},{20,16},{24,28},{28,24},{32,36},... | collective-permute-start | bytes 688136 | tf_op jit(solution)/shard_map/ppermute | solution.py:105
  138.7 17.7 %collective-permute-start.7 = (bf16[7,64,256]{2,1,0:T(8,128)(2,1)}, bf16[7,64,256]{2,1,0:T(8,128)(2,1)S(1)}, u32[]{:S(2)}, u32[]{:S(2)}) collective-permute-start(bf16[7,64,256]{2,1,0:T(8,128)(2,1)} %get-tuple-element.11), channel_id=1, source_target_pairs={{0,8},{4,12},{8,0},{12,4},{16,24},{20,28},{24,16},{28,20},{32,40},... | collective-permute-start | bytes 688136 | tf_op jit(solution)/shard_map/ppermute | solution.py:105
  141.0 20.1 %collective-permute-start.8 = (bf16[7,64,256]{2,1,0:T(8,128)(2,1)}, bf16[7,64,256]{2,1,0:T(8,128)(2,1)S(1)}, u32[]{:S(2)}, u32[]{:S(2)}) collective-permute-start(bf16[7,64,256]{2,1,0:T(8,128)(2,1)} %get-tuple-element.12), channel_id=1, source_target_pairs={{0,12},{4,8},{8,4},{12,0},{16,28},{20,24},{24,20},{28,16},{32,44},... | collective-permute-start | bytes 688136 | tf_op jit(solution)/shard_map/ppermute | solution.py:105
  144.6 16.5 %copy-start.2 = (bf16[7,64,256]{2,1,0:T(8,128)(2,1)}, bf16[7,64,256]{2,1,0:T(8,128)(2,1)S(1)}, u32[]{:S(2)}) copy-start(bf16[7,64,256]{2,1,0:T(8,128)(2,1)S(1)} %collective-permute-done.6.refs_1_) | copy-start | bytes 688132
  156.4 4.7 %copy-start.3 = (bf16[7,64,256]{2,1,0:T(8,128)(2,1)}, bf16[7,64,256]{2,1,0:T(8,128)(2,1)S(1)}, u32[]{:S(2)}) copy-start(bf16[7,64,256]{2,1,0:T(8,128)(2,1)S(1)} %collective-permute-done.7.refs_2_) | copy-start | bytes 688132
  161.1 0.7 copy-start.4
